TPU v7x, 128 devices: a whole 4x4x4 slice. The times are simulated.
128 devices in a mesh: row: 8 (over x, core), col: 16 (over z, y).
Axes of the slice: x: 4, y: 4, z: 4, core: 2. Of those that a mesh axis runs over, the one named last changes fastest.
Arguments:
- amplitudes: bfloat16 [16, 16, 512, 512], P(None, 'row', 'col'), may hold values from -6 to 6
- integrals: bfloat16 [16, 512, 16, 512], P('row', 'col'), may hold values from -0.09375 to 0.09375
- occupancy: int32 [16, 16, 4, 4], replicated, may hold values from 0 to 1, as said below
Outputs:
- cycle: bfloat16 [16, 16, 512, 512], P('col', 'row')
Inputs may be any that keep to these rules, and one draw needn't show every extreme that they name: occupancy[i, k, s, t] is 1 where tile s of the first virtual index and tile t of the second are kept for the pair (i, k), else 0; it is always 1 for i = k.
All inputs are finite; a program needn't handle non-finite values.
Results may differ from a plain program's by a relative error of at most 0.001.
Values may be sent and summed in bfloat16 or wider, within the bound.
No kernel may reach another device: no remote copies, remote signals or barrier semaphores. Data moves between devices by JAX's collectives and lax.ppermute only.
A program may use at most 128 MiB of HBM per device.

v0:
```python
import jax
import jax.numpy as jnp
from jax import lax
from jax.sharding import PartitionSpec as P

DOM = 4
TILE = 128


def screen(amplitudes, occupancy):
    k_rows = amplitudes.shape[1]
    c_rows = amplitudes.shape[2]
    k_first = lax.axis_index("row") * k_rows
    c_first = lax.axis_index("col") * c_rows
    occ_rows = lax.dynamic_slice_in_dim(occupancy, k_first, k_rows, 1).astype(jnp.float32)
    c_tiles = (c_first + jnp.arange(c_rows, dtype=jnp.int32)) // TILE
    picker = (c_tiles[:, None] == jnp.arange(DOM, dtype=jnp.int32)[None, :]).astype(jnp.float32)
    tile_rows = jnp.einsum("cs,ikst->ikct", picker, occ_rows)
    mask_full = jnp.repeat(tile_rows, TILE, axis=3).astype(jnp.bfloat16)
    return amplitudes * mask_full


def per_device(amplitudes, integrals, occupancy):
    screened = screen(amplitudes, occupancy)
    regrouped = lax.all_to_all(screened, "row", split_axis=0, concat_axis=1, tiled=True)
    turned = lax.all_to_all(integrals, "col", split_axis=2, concat_axis=1, tiled=True)
    complete = lax.all_gather(turned, "row", axis=0, tiled=True)
    summed = jnp.einsum(
        "ikca,kcjb->jiba",
        lax.all_gather(regrouped, "col", axis=2, tiled=True),
        complete,
        preferred_element_type=jnp.float32,
    )
    return summed.astype(jnp.bfloat16)


def solution(mesh):
    in_specs = (P(None, "row", "col", None), P("row", "col", None, None), P())
    out_specs = P("col", "row", None, None)
    return jax.shard_map(
        per_device, mesh=mesh, in_specs=in_specs, out_specs=out_specs, check_vma=False
    )
```

profile of v0, /device:TPU:1, one launch (start us, length us, event | category | flops | bytes accessed | tf_op | source)
XLA Modules:
  0.0 225.8 jit_solution(14420888662035065762)
XLA Ops:
  6.5 0.0 copy-start
  6.5 0.0 copy-start.1
  6.5 0.0 all-gather.5.cloned.1.call-start
  6.5 1.9 copy.17
  8.4 24.4 %all_to_all.36 = bf16[2,32,16,512]{3,1,0,2:T(8,128)(2,1)S(1)} all-to-all(bf16[2,32,16,512]{3,1,0,2:T(8,128)(2,1)S(1)} %copy.17), channel_id=1, replica_groups=mesh['row'=8,'col'=16] {'col'}, dimensions={2} | all-to-all | bytes 2097152 | tf_op jit(solution)/shard_map/all_to_all | solution.py:26
  32.9 1.1 copy.18
  34.0 0.0 all-gather.5.cloned.1.call-update
  34.0 0.0 all-gather.3.cloned.1.call-start
  34.1 0.0 copy-done
  34.1 0.1 constant_dynamic-slice_fusion
  34.2 0.2 copy.23
  34.4 0.2 fusion.7
  34.6 0.3 copy.15
  34.9 1.3 broadcast_in_dim.2
  36.2 0.4 convert_element_type.29
  36.6 0.0 copy-done.1
  36.6 0.4 mul.11
  37.0 32.1 %all_to_all.37 = bf16[16,2,32,512]{3,2,1,0:T(8,128)(2,1)S(1)} all-to-all(bf16[16,2,32,512]{3,2,1,0:T(8,128)(2,1)S(1)} %mul.11), channel_id=1, replica_groups=mesh['row'=8,'col'=16] {'row'}, dimensions={0} | all-to-all | bytes 2097152 | tf_op jit(solution)/shard_map/all_to_all | solution.py:25
  69.1 1.1 copy.16
  70.1 0.0 all-gather.3.cloned.1.call-update
  70.2 23.9 %all-gather.5.cloned.1.call-done = bf16[16,512,1,512]{3,1,2,0:T(8,128)(2,1)} async-done(((bf16[2,512,1,512]{3,1,2,0:T(8,128)(2,1)}), bf16[16,512,1,512]{3,1,2,0:T(8,128)(2,1)}) %all-gather.5.cloned.1.call-update) | async-done | bytes 8388624 | tf_op jit(solution)/shard_map/all_gather | solution.py:27
  94.1 108.7 %all-gather.3.cloned.1.call-done = bf16[2,16,512,512]{3,2,1,0:T(8,128)(2,1)} async-done(((bf16[2,16,32,512]{3,2,1,0:T(8,128)(2,1)}), bf16[2,16,512,512]{3,2,1,0:T(8,128)(2,1)}) %all-gather.3.cloned.1.call-update) | async-done | bytes 16777232 | tf_op jit(solution)/shard_map/all_gather | solution.py:30
  202.8 14.8 %fusion.4 = bf16[1,2,512,512]{2,3,1,0:T(8,128)(2,1)S(1)} fusion(bf16[2,16,512,512]{3,2,1,0:T(8,128)(2,1)} %all-gather.3.cloned.1.call-done, bf16[16,512,1,512]{3,1,2,0:T(8,128)(2,1)} %all-gather.5.cloned.1.call-done), kind=kOutput, calls=%fused_computation.3 | convolution fusion | flops 8590458880 | bytes 26214400 | tf_op jit(solution)/shard_map/ikca,kcjb->jiba/dot_general | solution.py:28
  217.6 1.3 copy.20
  (1 shorter events, 0.0 us)
Async XLA Ops:
  6.5 27.5 %copy-start = (s32[16,16,4,4]{1,3,2,0:T(4,128)S(1)}, s32[16,16,4,4]{1,3,2,0:T(4,128)}, u32[]{:S(2)}) copy-start(s32[16,16,4,4]{1,3,2,0:T(4,128)} %param.5) | copy-start | bytes 49156
  6.5 30.1 %copy-start.1 = (bf16[16,2,32,512]{3,2,1,0:T(8,128)(2,1)S(1)}, bf16[16,2,32,512]{3,2,1,0:T(8,128)(2,1)}, u32[]{:S(2)}) copy-start(bf16[16,2,32,512]{3,2,1,0:T(8,128)(2,1)} %param.3) | copy-start | bytes 3145732
  6.5 87.5 %all-gather.5.cloned.1.call-start = ((), (), s32[]{:S(2)}) async-start(), calls=%async_computation.3 | async-start | bytes 9437184 | tf_op jit(solution)/shard_map/all_gather | solution.py:27
  34.0 168.8 %all-gather.3.cloned.1.call-start = ((), (), s32[]{:S(2)}) async-start(), calls=%async_computation.2 | async-start | bytes 17825792 | tf_op jit(solution)/shard_map/all_gather | solution.py:30
Sparse Core Ops, SparseCore 0:
  34.1 59.8 all-gather.4
  96.2 106.5 all-gather.2
where the time goes:
time: 226 us
  waiting for transfers between devices  133 us (59%)
  blocking collectives  56.5 us (25%)
  matrix products  15 us (7%)
  between operations  13.5 us (6%)
  local copies, waits for them, and re-layouts  7.75 us (3%)
    all_gather x1, waiting for transfers between devices, per_device(): lax.all_gather(regrouped, 'col', axis=2, tiled=True)  109 us
    all_to_all x1, blocking collectives, per_device(): lax.all_to_all(screened, 'row', split_axis=0, concat_axis=1, tiled=True)  32.1 us
    all_to_all x1, blocking collectives, per_device(): lax.all_to_all(integrals, 'col', split_axis=2, concat_axis=1, tiled=True)  24.4 us
    all_gather x1, waiting for transfers between devices, per_device(): complete = lax.all_gather(turned, 'row', axis=0, tiled=True)  23.9 us
    dot_general x1, matrix products, per_device(): jnp.einsum('ikca,kcjb->jiba', lax.all_gather(regrouped, 'col', axis=2, ti...  14.8 us
  transfers between devices with their start and end apart: 2, of which 2 were waited for; matrix products, arithmetic and copies ran while one was open for 2% of the time, Pallas kernels for 0%

commit v1 on v0

--- a/solution.py
+++ b/solution.py
@@ -24,7 +24,10 @@
     screened = screen(amplitudes, occupancy)
     regrouped = lax.all_to_all(screened, "row", split_axis=0, concat_axis=1, tiled=True)
     turned = lax.all_to_all(integrals, "col", split_axis=2, concat_axis=1, tiled=True)
-    complete = lax.all_gather(turned, "row", axis=0, tiled=True)
+    size = lax.axis_size("row")
+    blocks = jnp.stack([turned for _ in range(size)])
+    blocks = lax.all_to_all(blocks, "row", split_axis=0, concat_axis=0)
+    complete = jnp.concatenate(blocks, axis=0)
     summed = jnp.einsum(
         "ikca,kcjb->jiba",
         lax.all_gather(regrouped, "col", axis=2, tiled=True),

time: 226 us -> 190 us (0.84)
  waiting for transfers between devices: 133 us -> 0.02 us
  blocking collectives: 56.5 us -> 153 us
    all_gather x1, waiting for transfers between devices: 109 us -> 0.01 us  [per_device(): lax.all_gather(regrouped, 'col', axis=2, tiled=True)]
    all_to_all x0 -> x1, blocking collectives: none -> 103 us  [per_device(): blocks = lax.all_to_all(blocks, 'row', split_axis=0, concat_axis=0)]
    all_gather x1 -> x0, waiting for transfers between devices: 23.9 us -> none  [per_device(): complete = lax.all_gather(turned, 'row', axis=0, tiled=True)]
    all_to_all x1, blocking collectives: 32.1 us -> 20.5 us  [per_device(): lax.all_to_all(screened, 'row', split_axis=0, concat_axis=1, tiled=True)]
    all_to_all x1, blocking collectives: 24.4 us -> 29.1 us  [per_device(): lax.all_to_all(integrals, 'col', split_axis=2, concat_axis=1, tiled=True)]
  transfers between devices with their start and end apart: 2 -> 1, of which waited for: 2 -> 0; matrix products, arithmetic and copies ran while one was open for 2% -> 1% of each run, Pallas kernels for 0% -> 0%
where the time goes in v1:
time: 190 us
  blocking collectives  153 us (81%)
  matrix products  15 us (8%)
  between operations  13.5 us (7%)
  local copies, waits for them, and re-layouts  7.04 us (4%)
    all_to_all x1, blocking collectives, per_device(): blocks = lax.all_to_all(blocks, 'row', split_axis=0, concat_axis=0)  103 us
    all_to_all x1, blocking collectives, per_device(): lax.all_to_all(integrals, 'col', split_axis=2, concat_axis=1, tiled=True)  29.1 us
    all_to_all x1, blocking collectives, per_device(): lax.all_to_all(screened, 'row', split_axis=0, concat_axis=1, tiled=True)  20.5 us
    dot_general x1, matrix products, per_device(): jnp.einsum('ikca,kcjb->jiba', lax.all_gather(regrouped, 'col', axis=2, ti...  14.8 us
  transfers between devices with their start and end apart: 1, of which 0 were waited for; matrix products, arithmetic and copies ran while one was open for 1% of the time, Pallas kernels for 0%

profile of v1, /device:TPU:1, one launch (start us, length us, event | category | flops | bytes accessed | tf_op | source)
XLA Modules:
  0.0 189.7 jit_solution(4514563984844290594)
XLA Ops:
  6.5 0.0 copy-start
  6.5 0.0 copy-start.1
  6.5 0.0 all-gather.2.cloned.1.call-start
  6.6 0.9 copy-done
  7.4 0.1 constant_dynamic-slice_fusion
  7.6 0.2 copy.21
  7.8 0.2 fusion.1
  8.0 0.3 copy.14
  8.3 1.3 broadcast_in_dim.2
  9.5 0.4 convert_element_type.29
  10.0 1.6 mul.11
  11.6 20.5 %all_to_all.38 = bf16[16,2,32,512]{3,2,1,0:T(8,128)(2,1)S(1)} all-to-all(bf16[16,2,32,512]{3,2,1,0:T(8,128)(2,1)S(1)} %mul.11), channel_id=1, replica_groups=mesh['row'=8,'col'=16] {'row'}, dimensions={0} | all-to-all | bytes 2097152 | tf_op jit(solution)/shard_map/all_to_all | solution.py:25
  32.1 1.0 copy.15
  33.1 0.0 all-gather.2.cloned.1.call-update
  33.2 0.0 copy-done.1
  33.2 0.6 copy.16
  33.8 29.1 %all_to_all.39 = bf16[2,32,16,512]{3,1,0,2:T(8,128)(2,1)S(1)} all-to-all(bf16[2,32,16,512]{3,1,0,2:T(8,128)(2,1)S(1)} %copy.16), channel_id=1, replica_groups=mesh['row'=8,'col'=16] {'col'}, dimensions={2} | all-to-all | bytes 2097152 | tf_op jit(solution)/shard_map/all_to_all | solution.py:26
  62.9 0.1 copy.17
  63.0 0.8 stack.5
  63.8 102.9 %all_to_all.40 = bf16[8,2,512,1,512]{4,2,1,3,0:T(8,128)(2,1)} all-to-all(bf16[8,2,512,1,512]{4,2,1,3,0:T(8,128)(2,1)S(1)} %stack.5), channel_id=1, replica_groups=mesh['row'=8,'col'=16] {'row'}, dimensions={0} | all-to-all | bytes 16777216 | tf_op jit(solution)/shard_map/all_to_all | solution.py:29
  166.7 0.0 all-gather.2.cloned.1.call-done
  166.7 14.8 %fusion = bf16[1,2,512,512]{2,3,1,0:T(8,128)(2,1)S(1)} fusion(bf16[2,16,512,512]{3,2,1,0:T(8,128)(2,1)} %all-gather.2.cloned.1.call-done, bf16[16,512,512,1]{2,1,0,3:T(8,128)(2,1)} %bitcast.32), kind=kOutput, calls=%fused_computation.1 | convolution fusion | flops 8590458880 | bytes 26214400 | tf_op jit(solution)/shard_map/ikca,kcjb->jiba/dot_general | solution.py:31
  181.5 1.3 copy.18
  (1 shorter events, 0.0 us)
Async XLA Ops:
  6.5 0.9 copy-start
  6.5 26.6 %copy-start.1 = (bf16[2,32,16,512]{3,2,1,0:T(8,128)(2,1)S(1)}, bf16[2,32,16,512]{3,2,1,0:T(8,128)(2,1)}, u32[]{:S(2)}) copy-start(bf16[2,32,16,512]{3,2,1,0:T(8,128)(2,1)} %param.4) | copy-start | bytes 3145732
  6.5 160.2 %all-gather.2.cloned.1.call-start = ((), (), s32[]{:S(2)}) async-start(), calls=%async_computation.3 | async-start | bytes 17825792 | tf_op jit(solution)/shard_map/all_gather | solution.py:33
Sparse Core Ops, SparseCore 0:
  33.3 117.0 all-gather.1
